TPU v7x, 768 devices: a whole 4x8x12 slice. The times are simulated.
768 devices in a mesh: worker: 16 (over x, y_lo, core), fsdp: 48 (over y_hi, z).
Axes of the slice: x: 4, y: 8 (y_hi: 4, y_lo: 2; y = y_hi * 2 + y_lo), z: 12, core: 2. Of those that a mesh axis runs over, the one named last changes fastest.
Arguments:
- queries: bfloat16 [196608, 2048], P(('worker', 'fsdp')), may hold values from -52 to 52
- key_states: bfloat16 [196608, 512], P(('worker', 'fsdp')), may hold values from -6 to 6
- value_states: bfloat16 [196608, 512], P(('worker', 'fsdp')), may hold values from -6 to 6
- output_grad: bfloat16 [196608, 2048], P(('worker', 'fsdp')), may hold values from -6 to 6
- key_blocks: int32 [1536, 2], P(('worker', 'fsdp')), may hold values from 0 to 15, as said below
- global_params: float32 [2, 3145728], P(None, 'fsdp'), may hold values from -6 to 6
- local_params: float32 [16, 3145728], P('worker', 'fsdp'), may hold values from -6 to 6
- momentum: float32 [2, 48, 16, 4096], P(None, 'fsdp', 'worker'), may hold values from -3 to 3
- fragment: int32 [1], replicated, may hold values from 0 to 1
Outputs:
- query_grad: bfloat16 [196608, 2048], P(('worker', 'fsdp'))
- key_grad: bfloat16 [196608, 512], P(('worker', 'fsdp'))
- value_grad: bfloat16 [196608, 512], P(('worker', 'fsdp'))
- new_params: float32 [2, 3145728], P(None, 'fsdp')
- new_momentum: float32 [2, 48, 16, 4096], P(None, 'fsdp', 'worker')
Inputs may be any that keep to these rules, and one draw needn't show every extreme that they name: `key_blocks`: entry 0 of each row is the row's own block index within its sequence; entry 1 is that index or the one before it.
All inputs are finite; a program needn't handle non-finite values.
Results may differ from a plain program's by a relative error of at most 0.005.
Values may be sent and summed in bfloat16 or wider, within the bound.
No kernel may reach another device: no remote copies, remote signals or barrier semaphores. Data moves between devices by JAX's collectives and lax.ppermute only.
A program may use at most 32 MiB of HBM per device.

v0:
```python
import math

import jax
import jax.numpy as jnp
from jax import lax
from jax.sharding import PartitionSpec as P

HEADS = 16
KV_HEADS = 4
HEAD_DIM = 128
BLOCK = 128
LENGTH = 2048


outer_rate = 0.7
outer_moment = 0.9


def from_behind(value, axis, steps):
    count = lax.axis_size(axis)
    initial, last = (max(0, -steps), min(count, count - steps))
    return lax.ppermute(value, axis, [(source, source + steps) for source in range(initial, last)])


def split_heads(states, head_width):
    count = states.shape[0]
    return jnp.moveaxis(states.reshape(count, KV_HEADS, -1, head_width), 1, 0)


def body(
    queries,
    key_states,
    value_states,
    output_grad,
    key_blocks,
    global_params,
    local_params,
    momentum,
    fragment,
):
    token_count = queries.shape[0]
    width = KV_HEADS * HEAD_DIM
    scaling = 1.0 / math.sqrt(HEAD_DIM)
    edge_from = token_count - BLOCK
    prev_keys, prev_values = from_behind(
        (key_states[edge_from:], value_states[edge_from:]), "fsdp", 1
    )
    all_keys = jnp.concatenate([prev_keys, key_states], 0)
    all_values = jnp.concatenate([prev_values, value_states], 0)
    start = lax.axis_index("fsdp") * token_count % LENGTH
    query_place = start + jnp.arange(token_count, dtype=jnp.int32)
    key_place = start - BLOCK + jnp.arange(token_count + BLOCK, dtype=jnp.int32)
    key_block = jnp.floor_divide(key_place, BLOCK)
    first_pick = jnp.repeat(key_blocks[:, 0], BLOCK)
    second_pick = jnp.repeat(key_blocks[:, 1], BLOCK)
    chosen = (key_block[None, :] == first_pick[:, None]) | (
        key_block[None, :] == second_pick[:, None]
    )
    allowed = chosen & (key_place[None, :] <= query_place[:, None])

    def group_grads(packed):
        query_part, grad_part, key_part, value_part = packed
        scores = (
            jnp.einsum("tgd,sd->gts", query_part, key_part, preferred_element_type=jnp.float32)
            * scaling
        )
        scores = jnp.where(allowed[None], scores, -jnp.inf)
        row_top = jnp.max(scores, -1, keepdims=True)
        log_total = row_top + jnp.log(jnp.sum(jnp.exp(scores - row_top), -1, keepdims=True))
        weights = jnp.exp(scores - log_total)
        weight_grad = jnp.einsum(
            "tgd,sd->gts", grad_part, value_part, preferred_element_type=jnp.float32
        )
        delta = jnp.sum(weights * weight_grad, -1, keepdims=True)
        score_grad = (weights * (weight_grad - delta) * scaling).astype(jnp.bfloat16)
        weights_low = weights.astype(jnp.bfloat16)
        query_out = jnp.einsum(
            "gts,sd->tgd", score_grad, key_part, preferred_element_type=jnp.float32
        )
        key_out = jnp.einsum(
            "gts,tgd->sd", score_grad, query_part, preferred_element_type=jnp.float32
        )
        value_out = jnp.einsum(
            "gts,tgd->sd", weights_low, grad_part, preferred_element_type=jnp.float32
        )
        return (query_out.astype(jnp.bfloat16), key_out, value_out)

    key_heads = jnp.moveaxis(all_keys.reshape(-1, KV_HEADS, HEAD_DIM), 1, 0)
    value_heads = jnp.moveaxis(all_values.reshape(-1, KV_HEADS, HEAD_DIM), 1, 0)
    query_groups, key_groups, value_groups = lax.map(
        group_grads,
        (
            split_heads(queries, HEAD_DIM),
            split_heads(output_grad, HEAD_DIM),
            key_heads,
            value_heads,
        ),
    )
    query_grad = jnp.moveaxis(query_groups, 0, 1).reshape(token_count, HEADS * HEAD_DIM)
    key_total = jnp.moveaxis(key_groups, 0, 1).reshape(token_count + BLOCK, width)
    value_total = jnp.moveaxis(value_groups, 0, 1).reshape(token_count + BLOCK, width)
    back_keys, back_values = from_behind((key_total[:BLOCK], value_total[:BLOCK]), "fsdp", -1)
    key_grad = jnp.concatenate(
        [key_total[BLOCK:token_count], key_total[token_count:] + back_keys], 0
    ).astype(jnp.bfloat16)
    value_grad = jnp.concatenate(
        [value_total[BLOCK:token_count], value_total[token_count:] + back_values], 0
    ).astype(jnp.bfloat16)
    slot_index = fragment[0]
    current = lax.dynamic_index_in_dim(global_params, slot_index, 0, keepdims=False)
    difference = current - local_params[0]
    moment = lax.dynamic_index_in_dim(momentum, slot_index, 0, keepdims=False).reshape(-1)
    workers = lax.axis_size("worker")
    share_len = current.shape[0] // workers
    share_start = lax.axis_index("worker") * share_len
    drift = lax.psum(difference, "worker") / workers
    drift_part = lax.dynamic_slice_in_dim(drift, share_start, share_len)
    new_moment = outer_moment * moment + drift_part
    full_moment = lax.all_gather(new_moment, "worker", axis=0, tiled=True)
    updated = current - outer_rate * (drift + outer_moment * full_moment)
    new_params = lax.dynamic_update_index_in_dim(global_params, updated, slot_index, 0)
    new_momentum = lax.dynamic_update_index_in_dim(
        momentum, new_moment.reshape(momentum.shape[1:]), slot_index, 0
    )
    return (query_grad, key_grad, value_grad, new_params, new_momentum)


def solution(mesh):
    placed = (
        P(("worker", "fsdp"), None),
        P(("worker", "fsdp"), None),
        P(("worker", "fsdp"), None),
        P(("worker", "fsdp"), None),
        P(("worker", "fsdp"), None),
        P(None, "fsdp"),
        P("worker", "fsdp"),
        P(None, "fsdp", "worker", None),
        P(),
    )
    return jax.shard_map(
        body,
        mesh=mesh,
        in_specs=placed,
        out_specs=(
            P(("worker", "fsdp"), None),
            P(("worker", "fsdp"), None),
            P(("worker", "fsdp"), None),
            P(None, "fsdp"),
            P(None, "fsdp", "worker", None),
        ),
        check_vma=False,
    )
```

profile of v0, /device:TPU:57, one launch (start us, length us, event | category | flops | bytes accessed | tf_op | source)
XLA Modules:
  0.0 209.5 jit_solution(1386741189017553110)
XLA Ops:
  11.5 4.0 %collective-permute-start = (bf16[128,512]{0,1:T(8,128)(2,1)}, bf16[128,512]{0,1:T(8,128)(2,1)}, u32[]{:S(2)}, u32[]{:S(2)}) collective-permute-start(bf16[128,512]{0,1:T(8,128)(2,1)} %slice.66), channel_id=1, source_target_pairs={{0,1},{1,2},{2,3},{3,4},{4,5},{5,6},{6,7},{7,8},{8,9},{9,10},{10,1... | collective-permute-start | bytes 393224 | tf_op jit(solution)/shard_map/ppermute | solution.py:22
  15.7 4.0 %collective-permute-start.1 = (bf16[128,512]{0,1:T(8,128)(2,1)S(1)}, bf16[128,512]{0,1:T(8,128)(2,1)}, u32[]{:S(2)}, u32[]{:S(2)}) collective-permute-start(bf16[128,512]{0,1:T(8,128)(2,1)S(1)} %slice.67), channel_id=1, source_target_pairs={{0,1},{1,2},{2,3},{3,4},{4,5},{5,6},{6,7},{7,8},{8,9},{9,10},{10,1... | collective-permute-start | bytes 393224 | tf_op jit(solution)/shard_map/ppermute | solution.py:22
  20.6 1.8 sub.41
  27.2 4.2 %collective-permute-done = bf16[128,512]{0,1:T(8,128)(2,1)} collective-permute-done((bf16[128,512]{0,1:T(8,128)(2,1)}, bf16[128,512]{0,1:T(8,128)(2,1)}, u32[]{:S(2)}, u32[]{:S(2)}) %collective-permute-start) | collective-permute-done | bytes 131104 | tf_op jit(solution)/shard_map/ppermute | solution.py:22
  31.4 1.7 pad_maximum_fusion
  33.2 3.6 %collective-permute-done.1 = bf16[128,512]{0,1:T(8,128)(2,1)} collective-permute-done((bf16[128,512]{0,1:T(8,128)(2,1)S(1)}, bf16[128,512]{0,1:T(8,128)(2,1)}, u32[]{:S(2)}, u32[]{:S(2)}) %collective-permute-start.1) | collective-permute-done | bytes 131104 | tf_op jit(solution)/shard_map/ppermute | solution.py:22
  36.8 1.7 pad_maximum_fusion.1
  38.5 42.7 %while.15 = (s32[]{:T(128)}, bf16[4,256,4,128]{1,3,2,0:T(8,128)(2,1)}, f32[4,384,128]{2,1,0:T(8,128)}, f32[4,384,128]{2,1,0:T(8,128)}, bf16[4,384,128]{1,2,0:T(8...) while((s32[]{:T(128)}, ...), condition=%wide.region_4.5_spmd.clone, body=%wide.region_0.4_spmd.clone.sunk | while | flops 512198400 | bytes 21126276 | solution.py:90
  39.3 1.4 fusion.74
  41.0 2.0 fusion.77
  43.0 1.4 fusion.73
  44.4 2.4 %fusion.76 = f32[4,384,128]{2,1,0:T(8,128)} fusion(f32[4,384,128]{2,1,0:T(8,128)} %get-tuple-element.253, s32[]{:T(128)} %get-tuple-element.251, f32[384,256,4]{1,0,2:T(8,128)S(1)} %fusion.73, f32[4,256,384]{1,2,0:T(8,128)S(1)} %get-tuple-element.235, f32[4,256]{1,0:T(4,128)S(1)} %log_add_fusion.2, bf16[4,256,4,128]{1,3,2,0:T(8,128)(2,1)} %get-tuple-element.270), kind=kOutput, calls=%fused_computation.19.clone.1 | convolution fusion | flops 103417216 | bytes 6759424 | tf_op jit(solution)/shard_map/while/body/eval_jaxpr/gts,tgd->sd/dot_general | solution.py:80
  46.8 2.4 %fusion.75 = bf16[4,256,4,128]{1,3,2,0:T(8,128)(2,1)} fusion(bf16[4,256,4,128]{1,3,2,0:T(8,128)(2,1)} %get-tuple-element.252, s32[]{:T(128)} %get-tuple-element.251, f32[384,256,4]{1,0,2:T(8,128)S(1)} %fusion.73, f32[4,256,384]{1,2,0:T(8,128)S(1)} %get-tuple-element.235, f32[4,256]{1,0:T(4,128)S(1)} %log_add_fusion.2, ...), kind=kOutput, calls=%fused_computation.15.clone.1 | convolution fusion | flops 103548288 | bytes 6661120 | tf_op jit(solution)/shard_map/while/body/eval_jaxpr/gts,sd->tgd/dot_general | solution.py:77
  50.0 1.4 fusion.74
  51.7 2.0 fusion.77
  53.7 1.4 fusion.73
  55.1 2.4 %fusion.76 = f32[4,384,128]{2,1,0:T(8,128)} fusion(f32[4,384,128]{2,1,0:T(8,128)} %get-tuple-element.253, s32[]{:T(128)} %get-tuple-element.251, f32[384,256,4]{1,0,2:T(8,128)S(1)} %fusion.73, f32[4,256,384]{1,2,0:T(8,128)S(1)} %get-tuple-element.235, f32[4,256]{1,0:T(4,128)S(1)} %log_add_fusion.2, bf16[4,256,4,128]{1,3,2,0:T(8,128)(2,1)} %get-tuple-element.270), kind=kOutput, calls=%fused_computation.19.clone.1 | convolution fusion | flops 103417216 | bytes 6759424 | tf_op jit(solution)/shard_map/while/body/eval_jaxpr/gts,tgd->sd/dot_general | solution.py:80
  57.4 2.4 %fusion.75 = bf16[4,256,4,128]{1,3,2,0:T(8,128)(2,1)} fusion(bf16[4,256,4,128]{1,3,2,0:T(8,128)(2,1)} %get-tuple-element.252, s32[]{:T(128)} %get-tuple-element.251, f32[384,256,4]{1,0,2:T(8,128)S(1)} %fusion.73, f32[4,256,384]{1,2,0:T(8,128)S(1)} %get-tuple-element.235, f32[4,256]{1,0:T(4,128)S(1)} %log_add_fusion.2, ...), kind=kOutput, calls=%fused_computation.15.clone.1 | convolution fusion | flops 103548288 | bytes 6661120 | tf_op jit(solution)/shard_map/while/body/eval_jaxpr/gts,sd->tgd/dot_general | solution.py:77
  60.7 1.4 fusion.74
  62.4 2.0 fusion.77
  65.8 2.3 %fusion.76 = f32[4,384,128]{2,1,0:T(8,128)} fusion(f32[4,384,128]{2,1,0:T(8,128)} %get-tuple-element.253, s32[]{:T(128)} %get-tuple-element.251, f32[384,256,4]{1,0,2:T(8,128)S(1)} %fusion.73, f32[4,256,384]{1,2,0:T(8,128)S(1)} %get-tuple-element.235, f32[4,256]{1,0:T(4,128)S(1)} %log_add_fusion.2, bf16[4,256,4,128]{1,3,2,0:T(8,128)(2,1)} %get-tuple-element.270), kind=kOutput, calls=%fused_computation.19.clone.1 | convolution fusion | flops 103417216 | bytes 6759424 | tf_op jit(solution)/shard_map/while/body/eval_jaxpr/gts,tgd->sd/dot_general | solution.py:80
  68.1 2.4 %fusion.75 = bf16[4,256,4,128]{1,3,2,0:T(8,128)(2,1)} fusion(bf16[4,256,4,128]{1,3,2,0:T(8,128)(2,1)} %get-tuple-element.252, s32[]{:T(128)} %get-tuple-element.251, f32[384,256,4]{1,0,2:T(8,128)S(1)} %fusion.73, f32[4,256,384]{1,2,0:T(8,128)S(1)} %get-tuple-element.235, f32[4,256]{1,0:T(4,128)S(1)} %log_add_fusion.2, ...), kind=kOutput, calls=%fused_computation.15.clone.1 | convolution fusion | flops 103548288 | bytes 6661120 | tf_op jit(solution)/shard_map/while/body/eval_jaxpr/gts,sd->tgd/dot_general | solution.py:77
  71.3 1.4 fusion.74
  73.0 2.0 fusion.77
  76.4 2.4 %fusion.76 = f32[4,384,128]{2,1,0:T(8,128)} fusion(f32[4,384,128]{2,1,0:T(8,128)} %get-tuple-element.253, s32[]{:T(128)} %get-tuple-element.251, f32[384,256,4]{1,0,2:T(8,128)S(1)} %fusion.73, f32[4,256,384]{1,2,0:T(8,128)S(1)} %get-tuple-element.235, f32[4,256]{1,0:T(4,128)S(1)} %log_add_fusion.2, bf16[4,256,4,128]{1,3,2,0:T(8,128)(2,1)} %get-tuple-element.270), kind=kOutput, calls=%fused_computation.19.clone.1 | convolution fusion | flops 103417216 | bytes 6759424 | tf_op jit(solution)/shard_map/while/body/eval_jaxpr/gts,tgd->sd/dot_general | solution.py:80
  78.8 2.4 %fusion.75 = bf16[4,256,4,128]{1,3,2,0:T(8,128)(2,1)} fusion(bf16[4,256,4,128]{1,3,2,0:T(8,128)(2,1)} %get-tuple-element.252, s32[]{:T(128)} %get-tuple-element.251, f32[384,256,4]{1,0,2:T(8,128)S(1)} %fusion.73, f32[4,256,384]{1,2,0:T(8,128)S(1)} %get-tuple-element.235, f32[4,256]{1,0:T(4,128)S(1)} %log_add_fusion.2, ...), kind=kOutput, calls=%fused_computation.15.clone.1 | convolution fusion | flops 103548288 | bytes 6661120 | tf_op jit(solution)/shard_map/while/body/eval_jaxpr/gts,sd->tgd/dot_general | solution.py:77
  84.1 3.9 %collective-permute-start.3 = (f32[128,512]{1,0:T(8,128)}, f32[128,512]{1,0:T(8,128)S(1)}, u32[]{:S(2)}, u32[]{:S(2)}) collective-permute-start(f32[128,512]{1,0:T(8,128)} %bitcast.144), channel_id=1, source_target_pairs={{1,0},{2,1},{3,2},{4,3},{5,4},{6,5},{7,6},{8,7},{9,8},{10,9},{11,1... | collective-permute-start | bytes 786440 | tf_op jit(solution)/shard_map/ppermute | solution.py:22
  88.0 3.4 %collective-permute-start.2 = (f32[128,512]{1,0:T(8,128)S(1)}, f32[128,512]{1,0:T(8,128)S(1)}, u32[]{:S(2)}, u32[]{:S(2)}) collective-permute-start(f32[128,512]{1,0:T(8,128)S(1)} %bitcast.185), channel_id=1, source_target_pairs={{1,0},{2,1},{3,2},{4,3},{5,4},{6,5},{7,6},{8,7},{9,8},{10,9},{11,1... | collective-permute-start | bytes 786440 | tf_op jit(solution)/shard_map/ppermute | solution.py:22
  91.4 1.4 copy.63
  92.9 81.2 %all-reduce.2.cloned.1.call-done = f32[65536]{0:T(1024)} async-done(((f32[65536]{0:T(1024)}), f32[65536]{0:T(1024)}) %all-reduce.2.cloned.1.call-update) | async-done | bytes 262160 | tf_op jit(solution)/shard_map/psum | solution.py:116
  175.1 21.7 %all_gather.3 = f32[65536]{0:T(1024)S(1)} all-gather(f32[4096]{0:T(1024)S(1)} %dynamic-slice_add_fusion), channel_id=1, replica_groups=mesh['worker'=16,'fsdp'=48] {'worker'}, dimensions={0}, use_global_device_ids=true | all-gather | bytes 278528 | tf_op jit(solution)/shard_map/all_gather | solution.py:119
  197.8 3.3 %dynamic_update_slice.19 = f32[2,65536]{1,0:T(2,128)S(1)} dynamic-update-slice(f32[2,65536]{1,0:T(2,128)S(1)} %copy-done.1, f32[1,65536]{1,0:T(1,128)S(1)} %bitcast.181, s32[]{:T(128)S(6)} %select_n.35, s32[]{:T(128)} %constant.75.clone.1) | dynamic-update-slice | bytes 524292 | tf_op jit(solution)/shard_map/jit(dynamic_update_index_in_dim)/dynamic_update_slice | solution.py:121
  (73 shorter events, 23.2 us)
Async XLA Ops:
  7.2 8.4 %copy-start.7 = (bf16[256,512]{1,0:T(8,128)(2,1)S(1)}, bf16[256,512]{1,0:T(8,128)(2,1)}, u32[]{:S(2)}) copy-start(bf16[256,512]{1,0:T(8,128)(2,1)} %param.13) | copy-start | bytes 786436
  7.2 166.9 %all-reduce.2.cloned.1.call-start = ((), (), s32[]{:S(2)}) async-start(), calls=%async_computation | async-start | bytes 524288 | tf_op jit(solution)/shard_map/psum | solution.py:116
  8.3 14.1 %copy-start = (f32[2,65536]{1,0:T(2,128)}, f32[2,65536]{1,0:T(2,128)S(1)}, u32[]{:S(2)}) copy-start(f32[2,65536]{1,0:T(2,128)S(1)} %copy.104) | copy-start | bytes 1572868
  9.7 12.8 %copy-start.11 = (s32[2,2]{1,0:T(2,128)S(1)}, s32[2,2]{1,0:T(2,128)}, u32[]{:S(2)}) copy-start(s32[2,2]{1,0:T(2,128)} %param.15) | copy-start | bytes 52
  9.7 14.9 %copy-start.3 = (bf16[256,2048]{1,0:T(8,128)(2,1)S(1)}, bf16[256,2048]{1,0:T(8,128)(2,1)}, u32[]{:S(2)}) copy-start(bf16[256,2048]{1,0:T(8,128)(2,1)} %param.11) | copy-start | bytes 3145732
  11.5 19.9 %collective-permute-start = (bf16[128,512]{0,1:T(8,128)(2,1)}, bf16[128,512]{0,1:T(8,128)(2,1)}, u32[]{:S(2)}, u32[]{:S(2)}) collective-permute-start(bf16[128,512]{0,1:T(8,128)(2,1)} %slice.66), channel_id=1, source_target_pairs={{0,1},{1,2},{2,3},{3,4},{4,5},{5,6},{6,7},{7,8},{8,9},{9,10},{10,1... | collective-permute-start | bytes 393224 | tf_op jit(solution)/shard_map/ppermute | solution.py:22
  15.7 21.1 %collective-permute-start.1 = (bf16[128,512]{0,1:T(8,128)(2,1)S(1)}, bf16[128,512]{0,1:T(8,128)(2,1)}, u32[]{:S(2)}, u32[]{:S(2)}) collective-permute-start(bf16[128,512]{0,1:T(8,128)(2,1)S(1)} %slice.67), channel_id=1, source_target_pairs={{0,1},{1,2},{2,3},{3,4},{4,5},{5,6},{6,7},{7,8},{8,9},{9,10},{10,1... | collective-permute-start | bytes 393224 | tf_op jit(solution)/shard_map/ppermute | solution.py:22
  20.6 5.3 %copy-start.4 = (bf16[256,2048]{1,0:T(8,128)(2,1)S(1)}, bf16[256,2048]{1,0:T(8,128)(2,1)}, u32[]{:S(2)}) copy-start(bf16[256,2048]{1,0:T(8,128)(2,1)} %param.14) | copy-start | bytes 3145732
  81.1 6.8 %copy-start.6 = (f32[4,384,128]{2,1,0:T(8,128)S(1)}, f32[4,384,128]{2,1,0:T(8,128)}, u32[]{:S(2)}) copy-start(f32[4,384,128]{2,1,0:T(8,128)} %get-tuple-element.55) | copy-start | bytes 2359300
  81.1 10.3 %copy-start.5 = (bf16[4,256,4,128]{1,3,2,0:T(8,128)(2,1)S(1)}, bf16[4,256,4,128]{1,3,2,0:T(8,128)(2,1)}, u32[]{:S(2)}) copy-start(bf16[4,256,4,128]{1,3,2,0:T(8,128)(2,1)} %get-tuple-element.54) | copy-start | bytes 3145732
  84.1 117.0 %collective-permute-start.3 = (f32[128,512]{1,0:T(8,128)}, f32[128,512]{1,0:T(8,128)S(1)}, u32[]{:S(2)}, u32[]{:S(2)}) collective-permute-start(f32[128,512]{1,0:T(8,128)} %bitcast.144), channel_id=1, source_target_pairs={{1,0},{2,1},{3,2},{4,3},{5,4},{6,5},{7,6},{8,7},{9,8},{10,9},{11,1... | collective-permute-start | bytes 786440 | tf_op jit(solution)/shard_map/ppermute | solution.py:22
  88.0 87.0 %copy-start.10 = (f32[1,1,1,4096]{3,2,1,0:T(1,128)S(1)}, f32[1,1,1,4096]{3,2,1,0:T(1,128)}, u32[]{:S(2)}) copy-start(f32[1,1,1,4096]{3,2,1,0:T(1,128)} %dynamic-slice_multiply_fusion) | copy-start | bytes 49156
  88.0 113.9 %collective-permute-start.2 = (f32[128,512]{1,0:T(8,128)S(1)}, f32[128,512]{1,0:T(8,128)S(1)}, u32[]{:S(2)}, u32[]{:S(2)}) collective-permute-start(f32[128,512]{1,0:T(8,128)S(1)} %bitcast.185), channel_id=1, source_target_pairs={{1,0},{2,1},{3,2},{4,3},{5,4},{6,5},{7,6},{8,7},{9,8},{10,9},{11,1... | collective-permute-start | bytes 786440 | tf_op jit(solution)/shard_map/ppermute | solution.py:22
  92.8 104.9 %copy-start.1 = (f32[2,65536]{1,0:T(2,128)S(1)}, f32[2,65536]{1,0:T(2,128)}, u32[]{:S(2)}) copy-start(f32[2,65536]{1,0:T(2,128)} %copy-done) | copy-start | bytes 1572868
  92.9 108.2 %copy-start.8 = (f32[2,1,1,4096]{3,2,1,0:T(1,128)S(1)}, f32[2,1,1,4096]{3,2,1,0:T(1,128)}, u32[]{:S(2)}) copy-start(f32[2,1,1,4096]{3,2,1,0:T(1,128)} %copy.105) | copy-start | bytes 98308
  201.1 1.6 copy-start.2
  201.1 1.6 copy-start.9
Sparse Core Ops, SparseCore 0:
  22.5 151.5 all-reduce.1
where the time goes:
time: 213 us; the launch traced here: 210 us
  waiting for transfers between devices  89.1 us (42%)
  matrix products  38.3 us (18%)
  blocking collectives  21.7 us (10%)
  starting transfers between devices  15.3 us (7%)
  local copies, waits for them, and re-layouts  15.2 us (7%)
  other arithmetic  15 us (7%)
  between operations  15 us (7%)
    psum x1, waiting for transfers between devices, body(): drift = lax.psum(difference, 'worker') / workers  81.2 us
    all_gather x1, blocking collectives, body(): full_moment = lax.all_gather(new_moment, 'worker', axis=0, tiled=True)  21.7 us
    ppermute x4, starting transfers between devices, from_behind(): lax.ppermute(value, axis, [(source, source + steps) for source in range(i...  15.2 us
    dot_general x4, matrix products, group_grads(): jnp.einsum('gts,sd->tgd', score_grad, key_part, preferred_element_type=jn...  9.57 us
    dot_general x4, matrix products, group_grads(): jnp.einsum('gts,tgd->sd', score_grad, query_part, preferred_element_type=...  9.42 us
    dot_general x4, matrix products, group_grads(): jnp.einsum('gts,tgd->sd', weights_low, grad_part, preferred_element_type=...  8.06 us
    ppermute x4, waiting for transfers between devices, from_behind(): lax.ppermute(value, axis, [(source, source + steps) for source in range(i...  7.82 us
    unnamed x32, local copies, waits for them, and re-layouts  7.65 us
  transfers between devices with their start and end apart: 5, of which 3 were waited for; matrix products, arithmetic and copies ran while one was open for 30% of the time, Pallas kernels for 0%

commit v1 on v0

v1 whole, which is shorter than its diff:
```python
import math

import jax
import jax.numpy as jnp
from jax import lax
from jax.experimental import pallas as pl
from jax.experimental.pallas import tpu as pltpu
from jax.sharding import PartitionSpec as P

HEADS = 16
KV_HEADS = 4
GROUP = HEADS // KV_HEADS
HEAD_DIM = 128
BLOCK = 128
LENGTH = 2048
LANES = 128

outer_rate = 0.7
outer_moment = 0.9

f32 = jnp.float32
bf16 = jnp.bfloat16
NEG = -jnp.inf


def dot(a, b, dims):
    return lax.dot_general(a, b, (dims, ((), ())), preferred_element_type=f32)


def attention_step(allow_prev, q, do, k, v):
    scaling = 1.0 / math.sqrt(HEAD_DIM)
    log2e = math.log2(math.e)
    q4 = jnp.concatenate([q[:, h * HEAD_DIM : (h + 1) * HEAD_DIM] for h in range(GROUP)], 0)
    do4 = jnp.concatenate([do[:, h * HEAD_DIM : (h + 1) * HEAD_DIM] for h in range(GROUP)], 0)
    cols = GROUP * BLOCK
    s = dot(k, q4, ((1,), (1,)))
    row = lax.broadcasted_iota(jnp.int32, (BLOCK, cols), 0)
    col = lax.broadcasted_iota(jnp.int32, (BLOCK, cols), 1) % BLOCK
    s_prev = jnp.where(allow_prev, s[:BLOCK], NEG)
    s_own = jnp.where(row <= col, s[BLOCK:], NEG)
    s = jnp.concatenate([s_prev, s_own], 0)
    top = jnp.max(s, 0, keepdims=True)
    p = jnp.exp2((s - top) * (scaling * log2e))
    total = jnp.sum(p, 0, keepdims=True)
    dp = dot(v, do4, ((1,), (1,)))
    w = p * (1.0 / total)
    delta = jnp.sum(w * dp, 0, keepdims=True)
    ds = ((w * scaling) * (dp - delta)).astype(bf16)
    w_low = w.astype(bf16)
    dk = dot(ds, q4, ((1,), (0,)))
    dv = dot(w_low, do4, ((1,), (0,)))
    dq_t = dot(k, ds, ((0,), (0,))).astype(bf16)
    dq = jnp.concatenate(
        [dq_t[:, h * BLOCK : (h + 1) * BLOCK].T for h in range(GROUP)], 1
    )
    return dq, dk, dv


def own_kernel(blocks_ref, q_ref, do_ref, k_ref, v_ref, dq_ref, dk0_ref, dv0_ref, dk1_ref, dv1_ref):
    allow_prev = blocks_ref[3] != blocks_ref[2]
    dq, dk, dv = attention_step(allow_prev, q_ref[...], do_ref[...], k_ref[...], v_ref[...])
    dq_ref[...] = dq
    dk0_ref[...] = dk[:BLOCK]
    dv0_ref[...] = dv[:BLOCK]
    dk1_ref[...] = dk[BLOCK:]
    dv1_ref[...] = dv[BLOCK:]


def edge_kernel(
    blocks_ref, q_ref, do_ref, k_ref, v_ref, halo_ref, dk0_ref, dv0_ref, dq_in,
    dq_ref, back_k_ref, back_v_ref, dk_ref, dv_ref,
):
    del dq_in
    allow_prev = blocks_ref[1] != blocks_ref[0]
    g = pl.program_id(0)
    width = HEAD_DIM * KV_HEADS
    kh = halo_ref[:, pl.ds(pl.multiple_of(g * HEAD_DIM, HEAD_DIM), HEAD_DIM)]
    vh = halo_ref[:, pl.ds(pl.multiple_of(width + g * HEAD_DIM, HEAD_DIM), HEAD_DIM)]
    k = jnp.concatenate([kh, k_ref[...]], 0)
    v = jnp.concatenate([vh, v_ref[...]], 0)
    dq, dk, dv = attention_step(allow_prev, q_ref[...], do_ref[...], k, v)
    dq_ref[...] = dq
    back_k_ref[...] = dk[:BLOCK].astype(bf16)
    back_v_ref[...] = dv[:BLOCK].astype(bf16)
    dk_ref[...] = (dk[BLOCK:] + dk0_ref[...]).astype(bf16)
    dv_ref[...] = (dv[BLOCK:] + dv0_ref[...]).astype(bf16)


def join_kernel(dk1_ref, dv1_ref, back_ref, dk_in, dv_in, dk_ref, dv_ref):
    del dk_in, dv_in
    width = dk1_ref.shape[1]
    dk_ref[...] = (dk1_ref[...] + back_ref[:, :width].astype(f32)).astype(bf16)
    dv_ref[...] = (dv1_ref[...] + back_ref[:, width:].astype(f32)).astype(bf16)


def outer_kernel(recv_ref, cur_ref, moment_ref, nm_ref, send_ref):
    workers = recv_ref.shape[0]
    cur = cur_ref[...]
    drift = cur - recv_ref[0]
    for w in range(1, workers):
        drift += cur - recv_ref[w]
    drift = drift / workers
    nm = outer_moment * moment_ref[...] + drift
    nm_ref[...] = nm
    upd = (cur - outer_rate * (drift + outer_moment * nm)).astype(bf16)
    for w in range(workers):
        send_ref[w] = upd


def body(
    queries,
    key_states,
    value_states,
    output_grad,
    key_blocks,
    global_params,
    local_params,
    momentum,
    fragment,
):
    width = KV_HEADS * HEAD_DIM
    gwidth = GROUP * HEAD_DIM
    workers = lax.axis_size("worker")
    count = lax.axis_size("fsdp")
    span = LENGTH // queries.shape[0]
    ahead = [(i, i + 1) for i in range(count - 1) if (i + 1) % span]
    behind = [(j, i) for i, j in ahead]
    blocks = key_blocks.reshape(-1)

    halo = lax.ppermute(
        jnp.concatenate([key_states[BLOCK:], value_states[BLOCK:]], 1), "fsdp", ahead
    )

    frag_len = global_params.shape[1]
    share = frag_len // workers
    rows = share // LANES
    slot = fragment[0]
    recv = lax.all_to_all(
        local_params.reshape(workers, rows, LANES), "worker", 0, 0, tiled=True
    )

    smem = pl.BlockSpec(memory_space=pltpu.SMEM)
    vmem = pl.BlockSpec(memory_space=pltpu.VMEM)
    kv_struct = jax.ShapeDtypeStruct((BLOCK, width), f32)
    kv_spec = pl.BlockSpec((BLOCK, HEAD_DIM), lambda g: (0, g))
    est = pl.CostEstimate(
        flops=5 * 2 * HEADS * BLOCK * 2 * BLOCK * HEAD_DIM,
        bytes_accessed=2 * 1024 * 1024,
        transcendentals=HEADS * BLOCK * 2 * BLOCK,
    )
    dq, dk0, dv0, dk1, dv1 = pl.pallas_call(
        own_kernel,
        grid=(KV_HEADS,),
        in_specs=[
            smem,
            pl.BlockSpec((BLOCK, gwidth), lambda g: (1, g)),
            pl.BlockSpec((BLOCK, gwidth), lambda g: (1, g)),
            pl.BlockSpec((2 * BLOCK, HEAD_DIM), lambda g: (0, g)),
            pl.BlockSpec((2 * BLOCK, HEAD_DIM), lambda g: (0, g)),
        ],
        out_specs=[pl.BlockSpec((BLOCK, gwidth), lambda g: (1, g)), kv_spec, kv_spec, kv_spec, kv_spec],
        out_shape=[jax.ShapeDtypeStruct(queries.shape, bf16), kv_struct, kv_struct, kv_struct, kv_struct],
        cost_estimate=est,
        compiler_params=pltpu.CompilerParams(vmem_limit_bytes=16 << 20),
        name="attn_own",
    )(blocks, queries, output_grad, key_states, value_states)

    query_grad, back_k, back_v, key_grad, value_grad = pl.pallas_call(
        edge_kernel,
        grid=(KV_HEADS,),
        in_specs=[
            smem,
            pl.BlockSpec((BLOCK, gwidth), lambda g: (0, g)),
            pl.BlockSpec((BLOCK, gwidth), lambda g: (0, g)),
            kv_spec,
            kv_spec,
            vmem,
            kv_spec,
            kv_spec,
            pl.BlockSpec(memory_space=pl.ANY),
        ],
        out_specs=[
            pl.BlockSpec((BLOCK, gwidth), lambda g: (0, g)),
            kv_spec,
            kv_spec,
            kv_spec,
            kv_spec,
        ],
        out_shape=[
            jax.ShapeDtypeStruct(queries.shape, bf16),
            jax.ShapeDtypeStruct((BLOCK, width), bf16),
            jax.ShapeDtypeStruct((BLOCK, width), bf16),
            jax.ShapeDtypeStruct(key_states.shape, bf16),
            jax.ShapeDtypeStruct(value_states.shape, bf16),
        ],
        input_output_aliases={8: 0},
        cost_estimate=est,
        compiler_params=pltpu.CompilerParams(vmem_limit_bytes=16 << 20),
        name="attn_edge",
    )(blocks, queries, output_grad, key_states, value_states, halo, dk0, dv0, dq)

    back = lax.ppermute(jnp.concatenate([back_k, back_v], 1), "fsdp", behind)

    start = lax.axis_index("worker") * share
    cur = lax.dynamic_slice(global_params, (slot, start), (1, share)).reshape(rows, LANES)
    moment = lax.dynamic_index_in_dim(momentum, slot, 0, keepdims=False).reshape(rows, LANES)
    new_moment, send = pl.pallas_call(
        outer_kernel,
        out_shape=[
            jax.ShapeDtypeStruct((rows, LANES), f32),
            jax.ShapeDtypeStruct((workers, rows, LANES), bf16),
        ],
        in_specs=[vmem] * 3,
        out_specs=[vmem] * 2,
        compiler_params=pltpu.CompilerParams(vmem_limit_bytes=8 << 20),
        name="outer",
    )(recv, cur, moment)
    updated = lax.all_to_all(send, "worker", 0, 0, tiled=True).reshape(1, frag_len)
    picked = lax.broadcasted_iota(jnp.int32, global_params.shape, 0) == slot
    new_params = jnp.where(picked, updated.astype(f32), global_params)
    new_momentum = lax.dynamic_update_index_in_dim(
        momentum, new_moment.reshape(momentum.shape[1:]), slot, 0
    )

    half_spec = pl.BlockSpec((BLOCK, width), lambda i: (0, 0))
    key_grad, value_grad = pl.pallas_call(
        join_kernel,
        grid=(1,),
        in_specs=[
            half_spec,
            half_spec,
            vmem,
            pl.BlockSpec(memory_space=pl.ANY),
            pl.BlockSpec(memory_space=pl.ANY),
        ],
        out_specs=[pl.BlockSpec((BLOCK, width), lambda i: (1, 0))] * 2,
        out_shape=[
            jax.ShapeDtypeStruct(key_states.shape, bf16),
            jax.ShapeDtypeStruct(value_states.shape, bf16),
        ],
        input_output_aliases={3: 0, 4: 1},
        compiler_params=pltpu.CompilerParams(vmem_limit_bytes=8 << 20),
        name="join",
    )(dk1, dv1, back, key_grad, value_grad)
    return (query_grad, key_grad, value_grad, new_params, new_momentum)


def solution(mesh):
    placed = (
        P(("worker", "fsdp"), None),
        P(("worker", "fsdp"), None),
        P(("worker", "fsdp"), None),
        P(("worker", "fsdp"), None),
        P(("worker", "fsdp"), None),
        P(None, "fsdp"),
        P("worker", "fsdp"),
        P(None, "fsdp", "worker", None),
        P(),
    )
    return jax.shard_map(
        body,
        mesh=mesh,
        in_specs=placed,
        out_specs=(
            P(("worker", "fsdp"), None),
            P(("worker", "fsdp"), None),
            P(("worker", "fsdp"), None),
            P(None, "fsdp"),
            P(None, "fsdp", "worker", None),
        ),
        check_vma=False,
    )
```

time: 213 us -> 54.4 us (0.26); the launches traced: 210 us -> 53.9 us
  waiting for transfers between devices: 89.1 us -> 10.9 us
  matrix products: 38.3 us -> 0 us
  blocking collectives: 21.7 us -> 0 us
  other arithmetic: 15 us -> 1.19 us
  between operations: 15 us -> 1.44 us
  Pallas kernels: 0 us -> 11.2 us
  local copies, waits for them, and re-layouts: 15.2 us -> 5.54 us
  starting transfers between devices: 15.3 us -> 23.6 us
    psum x1 -> x0, waiting for transfers between devices: 81.2 us -> none  [body(): drift = lax.psum(difference, 'worker') / workers]
    dot_general x20 -> x0, matrix products: 38.3 us -> none  [the longest x4 9.57 us: group_grads(): jnp.einsum('gts,sd->tgd', score_grad, key_part, preferred_element_type=jn...]
    all_gather x1 -> x0, blocking collectives: 21.7 us -> none  [body(): full_moment = lax.all_gather(new_moment, 'worker', axis=0, tiled=True)]
    all_to_all x0 -> x2, starting transfers between devices: none -> 12.5 us  [the longest x1 6.48 us: body(): lax.all_to_all(local_params.reshape(workers, rows, LANES), 'worker', 0, 0...]
    pallas_call x0 -> x4, Pallas kernels: none -> 11.2 us  [the longest x1 4.88 us: body(): pl.pallas_call(edge_kernel, grid=(KV_HEADS,), in_specs=[smem, pl.BlockSpe...]
    unnamed x32 -> x15, local copies, waits for them, and re-layouts: 7.65 us -> 2.76 us
    concatenate x4 -> x2, other arithmetic: 4.92 us -> 0.04 us  [the longest x1 0.02 us: body(): jnp.concatenate([key_states[BLOCK:], value_states[BLOCK:]], 1)]
    all_to_all x0 -> x2, waiting for transfers between devices: none -> 4.08 us  [the longest x1 4.07 us: body(): lax.all_to_all(send, 'worker', 0, 0, tiled=True).reshape(1, frag_len)]
  transfers between devices with their start and end apart: 5 -> 4, of which waited for: 3 -> 3; matrix products, arithmetic and copies ran while one was open for 30% -> 2% of each run, Pallas kernels for 0% -> 21%
where the time goes in v1:
time: 54.4 us; the launch traced here: 53.9 us
  starting transfers between devices  23.6 us (43%)
  Pallas kernels  11.2 us (21%)
  waiting for transfers between devices  10.9 us (20%)
  local copies, waits for them, and re-layouts  5.54 us (10%)
  between operations  1.44 us (3%)
  other arithmetic  1.19 us (2%)
    ppermute x1, starting transfers between devices, body(): back = lax.ppermute(jnp.concatenate([back_k, back_v], 1), 'fsdp', behind)  7.19 us
    all_to_all x1, starting transfers between devices, body(): lax.all_to_all(local_params.reshape(workers, rows, LANES), 'worker', 0, 0...  6.48 us
    ppermute x1, waiting for transfers between devices, body(): lax.ppermute(jnp.concatenate([key_states[BLOCK:], value_states[BLOCK:]],...  6.39 us
    all_to_all x1, starting transfers between devices, body(): lax.all_to_all(send, 'worker', 0, 0, tiled=True).reshape(1, frag_len)  5.98 us
    pallas_call x1, Pallas kernels, body(): pl.pallas_call(edge_kernel, grid=(KV_HEADS,), in_specs=[smem, pl.BlockSpe...  4.88 us
    pallas_call x1, Pallas kernels, body(): pl.pallas_call(own_kernel, grid=(KV_HEADS,), in_specs=[smem, pl.BlockSpec...  4.85 us
    all_to_all x1, waiting for transfers between devices, body(): lax.all_to_all(send, 'worker', 0, 0, tiled=True).reshape(1, frag_len)  4.07 us
    ppermute x1, starting transfers between devices, body(): lax.ppermute(jnp.concatenate([key_states[BLOCK:], value_states[BLOCK:]],...  4 us
  transfers between devices with their start and end apart: 4, of which 3 were waited for; matrix products, arithmetic and copies ran while one was open for 2% of the time, Pallas kernels for 21%

profile of v1, /device:TPU:57, one launch (start us, length us, event | category | flops | bytes accessed | tf_op | source)
XLA Modules:
  0.0 53.9 jit_solution(4574917853994105279)
XLA Ops:
  0.6 0.0 copy-start
  0.6 0.8 %copy.23 = f32[2,1,1,4096]{3,2,1,0:T(1,128)S(1)} copy(f32[2,1,1,4096]{3,2,1,0:T(1,128)} %param.16) | data formatting | bytes 65536
  1.5 0.9 %slice.6 = bf16[128,512]{1,0:T(8,128)(2,1)S(1)} slice(bf16[256,512]{1,0:T(8,128)(2,1)} %k_ref.3), slice={[128:256], [0:512]} | slice | bytes 262144 | tf_op jit(solution)/shard_map/slice | solution.py:131
  2.4 0.9 %slice.7 = bf16[128,512]{1,0:T(8,128)(2,1)S(1)} slice(bf16[256,512]{1,0:T(8,128)(2,1)} %v_ref.3), slice={[128:256], [0:512]} | slice | bytes 262144 | tf_op jit(solution)/shard_map/slice | solution.py:131
  3.4 4.0 %collective-permute-start = (bf16[128,1024]{1,0:T(8,128)(2,1)S(1)}, bf16[128,1024]{1,0:T(8,128)(2,1)S(1)}, u32[]{:S(2)}, u32[]{:S(2)}) collective-permute-start(bf16[128,1024]{1,0:T(8,128)(2,1)S(1)} %pad_maximum_fusion), channel_id=1, source_target_pairs={{0,1},{1,2},{2,3},{3,4},{4,5},{5,6},{6,7},{8,9},{9,10},{10,11},{11... | collective-permute-start | bytes 786440 | tf_op jit(solution)/shard_map/ppermute | solution.py:130
  7.4 0.0 copy-start.2
  7.4 0.0 copy-start.3
  7.4 6.5 %all-to-all-start = ((f32[16,32,128]{2,1,0:T(8,128)}), f32[16,32,128]{2,1,0:T(8,128)S(1)}, u32[]{:S(2)}, u32[]{:S(2)}) async-start(f32[16,32,128]{2,1,0:T(8,128)} %bitcast.15), calls=%async_computation | async-start | bytes 524288 | tf_op jit(solution)/shard_map/all_to_all | solution.py:138
  14.5 0.0 copy-start.6
  14.6 0.7 %copy-done.6 = s32[2,2]{1,0:T(2,128)S(1)} copy-done((s32[2,2]{1,0:T(2,128)S(1)}, s32[2,2]{1,0:T(2,128)}, u32[]{:S(2)}) %copy-start.6) | copy-done | bytes 40
  15.2 0.1 reshape.35.blocks_ref
  15.3 0.8 %dynamic_slice.7 = f32[1,4096]{1,0:T(1,128)S(1)} dynamic-slice(f32[2,65536]{1,0:T(2,128)} %param.14, s32[]{:T(128)S(6)} %select_n.14, s32[]{:T(128)S(6)} %select_n.15), dynamic_slice_sizes={1,4096} | dynamic-slice | bytes 32772 | tf_op jit(solution)/shard_map/dynamic_slice | solution.py:205
  16.2 0.0 copy-done
  16.2 0.0 copy-done.2
  16.2 0.0 copy-done.3
  16.2 0.0 copy-start.1
  16.2 1.2 %copy-done.1 = bf16[256,2048]{1,0:T(8,128)(2,1)S(1)} copy-done((bf16[256,2048]{1,0:T(8,128)(2,1)S(1)}, bf16[256,2048]{1,0:T(8,128)(2,1)}, u32[]{:S(2)}) %copy-start.1) | copy-done | bytes 1048600
  17.4 4.8 %attn_own.1 = (bf16[256,2048]{1,0:T(8,128)(2,1)}, f32[128,512]{1,0:T(8,128)S(1)}, f32[128,512]{1,0:T(8,128)S(1)}, f32[128,512]{1,0:T(8,128)S(1)}, f32[128,512]{1,0:T(8,128)S(1)}) custom-call(s32[4]{0:T(128)S(1)} %reshape.35.blocks_ref, bf16[256,2048]{1,0:T(8,128)(2,1)S(1)} %copy-done, bf16[256,2048]{1,0:T(8,128)(2,1)S(1)} %copy-done.1, ...), custom_call_target="tpu_custom_call" | custom-call | flops 671088640 | bytes 2097152 | tf_op jit(solution)/shard_map/attn_own/pallas_call | solution.py:151
  22.3 6.4 %collective-permute-done.halo_ref = bf16[128,1024]{1,0:T(8,128)(2,1)S(1)} collective-permute-done((bf16[128,1024]{1,0:T(8,128)(2,1)S(1)}, bf16[128,1024]{1,0:T(8,128)(2,1)S(1)}, u32[]{:S(2)}, u32[]{:S(2)}) %collective-permute-start) | collective-permute-done | bytes 262176 | tf_op jit(solution)/shard_map/ppermute | solution.py:130
  28.7 4.9 %attn_edge.1 = (bf16[256,2048]{1,0:T(8,128)(2,1)}, bf16[128,512]{1,0:T(8,128)(2,1)S(1)}, bf16[128,512]{1,0:T(8,128)(2,1)S(1)}, bf16[256,512]{1,0:T(8,128)(2,1)}, bf16[256,512]{1,0:T(8,128)(2,1)}) custom-call(s32[4]{0:T(128)S(1)} %reshape.35.blocks_ref, bf16[256,2048]{1,0:T(8,128)(2,1)S(1)} %copy-done, ...), custom_call_target="tpu_custom_call", output_to_operand_aliasing={{0}: (8, {})} | custom-call | flops 671088640 | bytes 2097152 | tf_op jit(solution)/shard_map/attn_edge/pallas_call | solution.py:168
  33.6 7.2 %collective-permute-start.1 = (bf16[128,1024]{1,0:T(8,128)(2,1)S(1)}, bf16[128,1024]{1,0:T(8,128)(2,1)S(1)}, u32[]{:S(2)}, u32[]{:S(2)}) collective-permute-start(bf16[128,1024]{1,0:T(8,128)(2,1)S(1)} %pad_maximum_fusion.1), channel_id=1, source_target_pairs={{1,0},{2,1},{3,2},{4,3},{5,4},{6,5},{7,6},{9,8},{10,9},{11,10},{12... | collective-permute-start | bytes 786440 | tf_op jit(solution)/shard_map/ppermute | solution.py:202
  40.8 0.0 all-to-all-done.recv_ref
  40.8 0.7 %outer.1 = (f32[32,128]{1,0:T(8,128)S(1)}, bf16[16,32,128]{2,1,0:T(8,128)(2,1)}) custom-call(f32[16,32,128]{2,1,0:T(8,128)S(1)} %all-to-all-done.recv_ref, f32[32,128]{1,0:T(8,128)S(1)} %bitcast.12, f32[32,128]{1,0:T(8,128)S(1)} %bitcast.11), custom_call_target="tpu_custom_call" | custom-call | tf_op jit(solution)/shard_map/outer/pallas_call | solution.py:207
  41.5 6.0 %all-to-all-start.1 = ((bf16[16,32,128]{2,1,0:T(8,128)(2,1)}), bf16[16,32,128]{2,1,0:T(8,128)(2,1)S(1)}, u32[]{:S(2)}, u32[]{:S(2)}) async-start(bf16[16,32,128]{2,1,0:T(8,128)(2,1)} %get-tuple-element.31), calls=%async_computation.1 | async-start | bytes 262144 | tf_op jit(solution)/shard_map/all_to_all | solution.py:218
  47.5 0.0 copy-start.5
  47.5 0.4 collective-permute-done.1.back_ref
  47.9 0.0 copy-start.4
  47.9 0.7 %join.1 = (bf16[256,512]{1,0:T(8,128)(2,1)}, bf16[256,512]{1,0:T(8,128)(2,1)}) custom-call(f32[128,512]{1,0:T(8,128)S(1)} %get-tuple-element.23.dk1_ref, f32[128,512]{1,0:T(8,128)S(1)} %get-tuple-element.24.dv1_ref, bf16[128,1024]{1,0:T(8,128)(2,1)S(1)} %collective-permute-done.1.back_ref, ...), custom_call_target="tpu_custom_call", output_to_operand_aliasing={{0}: (3, {}), {1}: (4, {})} | custom-call | tf_op jit(solution)/shard_map/join/pallas_call | solution.py:226
  48.6 0.0 copy-done.5
  48.6 4.1 %all-to-all-done.1 = bf16[16,32,128]{2,1,0:T(8,128)(2,1)S(1)} async-done(((bf16[16,32,128]{2,1,0:T(8,128)(2,1)}), bf16[16,32,128]{2,1,0:T(8,128)(2,1)S(1)}, u32[]{:S(2)}, u32[]{:S(2)}) %all-to-all-start.1) | async-done | bytes 131104 | tf_op jit(solution)/shard_map/all_to_all | solution.py:218
  52.7 0.0 copy-done.4
  52.7 1.1 %broadcast_select_fusion = f32[2,65536]{1,0:T(2,128)} fusion(f32[2,65536]{1,0:T(2,128)S(1)} %copy-done.4, pred[2]{0:T(512)(128)(4,1)S(1)} %iota_compare_fusion, f32[65536]{0:T(1024)S(1)} %convert.1), kind=kLoop, calls=%fused_computation | loop fusion | flops 131072 | bytes 1310722 | tf_op jit(solution)/shard_map/jit(_where)/select_n | solution.py:220
  (6 shorter events, 0.1 us)
Async XLA Ops:
  0.6 15.5 %copy-start = (bf16[256,2048]{1,0:T(8,128)(2,1)S(1)}, bf16[256,2048]{1,0:T(8,128)(2,1)}, u32[]{:S(2)}) copy-start(bf16[256,2048]{1,0:T(8,128)(2,1)} %q_ref.3) | copy-start | bytes 3145732
  3.4 25.3 %collective-permute-start = (bf16[128,1024]{1,0:T(8,128)(2,1)S(1)}, bf16[128,1024]{1,0:T(8,128)(2,1)S(1)}, u32[]{:S(2)}, u32[]{:S(2)}) collective-permute-start(bf16[128,1024]{1,0:T(8,128)(2,1)S(1)} %pad_maximum_fusion), channel_id=1, source_target_pairs={{0,1},{1,2},{2,3},{3,4},{4,5},{5,6},{6,7},{8,9},{9,10},{10,11},{11... | collective-permute-start | bytes 786440 | tf_op jit(solution)/shard_map/ppermute | solution.py:130
  7.4 8.8 %copy-start.2 = (bf16[256,512]{1,0:T(8,128)(2,1)S(1)}, bf16[256,512]{1,0:T(8,128)(2,1)}, u32[]{:S(2)}) copy-start(bf16[256,512]{1,0:T(8,128)(2,1)} %k_ref.3) | copy-start | bytes 786436
  7.4 8.8 %copy-start.3 = (bf16[256,512]{1,0:T(8,128)(2,1)S(1)}, bf16[256,512]{1,0:T(8,128)(2,1)}, u32[]{:S(2)}) copy-start(bf16[256,512]{1,0:T(8,128)(2,1)} %v_ref.3) | copy-start | bytes 786436
  7.4 33.4 %all-to-all-start = ((f32[16,32,128]{2,1,0:T(8,128)}), f32[16,32,128]{2,1,0:T(8,128)S(1)}, u32[]{:S(2)}, u32[]{:S(2)}) async-start(f32[16,32,128]{2,1,0:T(8,128)} %bitcast.15), calls=%async_computation | async-start | bytes 524288 | tf_op jit(solution)/shard_map/all_to_all | solution.py:138
  14.5 0.7 %copy-start.6 = (s32[2,2]{1,0:T(2,128)S(1)}, s32[2,2]{1,0:T(2,128)}, u32[]{:S(2)}) copy-start(s32[2,2]{1,0:T(2,128)} %param.13) | copy-start | bytes 52
  16.2 1.2 %copy-start.1 = (bf16[256,2048]{1,0:T(8,128)(2,1)S(1)}, bf16[256,2048]{1,0:T(8,128)(2,1)}, u32[]{:S(2)}) copy-start(bf16[256,2048]{1,0:T(8,128)(2,1)} %do_ref.3) | copy-start | bytes 3145732
  33.6 14.3 %collective-permute-start.1 = (bf16[128,1024]{1,0:T(8,128)(2,1)S(1)}, bf16[128,1024]{1,0:T(8,128)(2,1)S(1)}, u32[]{:S(2)}, u32[]{:S(2)}) collective-permute-start(bf16[128,1024]{1,0:T(8,128)(2,1)S(1)} %pad_maximum_fusion.1), channel_id=1, source_target_pairs={{1,0},{2,1},{3,2},{4,3},{5,4},{6,5},{7,6},{9,8},{10,9},{11,10},{12... | collective-permute-start | bytes 786440 | tf_op jit(solution)/shard_map/ppermute | solution.py:202
  41.5 11.2 %all-to-all-start.1 = ((bf16[16,32,128]{2,1,0:T(8,128)(2,1)}), bf16[16,32,128]{2,1,0:T(8,128)(2,1)S(1)}, u32[]{:S(2)}, u32[]{:S(2)}) async-start(bf16[16,32,128]{2,1,0:T(8,128)(2,1)} %get-tuple-element.31), calls=%async_computation.1 | async-start | bytes 262144 | tf_op jit(solution)/shard_map/all_to_all | solution.py:218
  47.5 1.2 %copy-start.5 = (f32[2,1,1,4096]{3,2,1,0:T(1,128)}, f32[2,1,1,4096]{3,2,1,0:T(1,128)S(1)}, u32[]{:S(2)}) copy-start(f32[2,1,1,4096]{3,2,1,0:T(1,128)S(1)} %constant_dynamic-update-slice_fusion) | copy-start | bytes 98308
  47.9 4.8 %copy-start.4 = (f32[2,65536]{1,0:T(2,128)S(1)}, f32[2,65536]{1,0:T(2,128)}, u32[]{:S(2)}) copy-start(f32[2,65536]{1,0:T(2,128)} %param.14) | copy-start | bytes 1572868
